TPU v7x, 32 devices: a whole 2x2x4 slice. The times are simulated.
32 devices in a mesh: group: 2 (over y), frame: 8 (over z, x), row: 2 (over core).
Axes of the slice: x: 2, y: 2, z: 4, core: 2. Of those that a mesh axis runs over, the one named last changes fastest.
Arguments:
- latents: bfloat16 [16, 8, 32, 1120], P(('group', 'frame'), 'row'), parts along dimension 0, may hold values from -24 to 24
- spatial_weights: bfloat16 [4, 10, 112, 112], replicated, may hold values from -0.5 to 0.5
- causal_weights: bfloat16 [4, 10, 112, 112], replicated, may hold values from -0.5 to 0.5
Outputs:
- updated_latents: bfloat16 [16, 8, 32, 1120], P(('group', 'frame'), None, None, 'row'), parts along dimension 0
There are 2 independent parts, one for each index of `group`. A program takes and returns all parts, laid end to end along the dimension named above; an argument that names none is the same for every part. Nothing has to cross between parts.
All inputs are finite; a program needn't handle non-finite values.
Results may differ from a plain program's by a relative error of at most 0.0047.
The roundings to bfloat16 on the way count: a program that leaves them out, or rounds other values in their place, can miss the bound.
Values may be sent and summed in bfloat16 or wider, within the bound.
No kernel may reach another device: no remote copies, remote signals or barrier semaphores. Data moves between devices by JAX's collectives and lax.ppermute only.
A program may use at most 64 MiB of HBM per device.

v0:
```python
import jax
import jax.numpy as jnp
from jax import lax
from jax.sharding import PartitionSpec as P


def prefix(x, axis, join, neutral):
    place = lax.axis_index(axis)
    gathered = lax.all_gather(x.astype(jnp.bfloat16), axis)
    state = jnp.zeros_like(x) + jnp.asarray(neutral, x.dtype)

    def one(turn, state):
        return join(state, lax.dynamic_index_in_dim(gathered, turn, 0, False).astype(x.dtype))

    return lax.fori_loop(0, place, one, state)


def normalize(frame_block):
    feat_width = frame_block.shape[-1]
    flat_rows = frame_block.reshape(-1, feat_width).astype(jnp.float32)
    normed = flat_rows * lax.rsqrt(jnp.mean(flat_rows * flat_rows, axis=-1, keepdims=True) + 1e-06)
    return normed.astype(jnp.bfloat16).reshape(frame_block.shape)


def project(normed, weights):
    head_count = weights.shape[1]
    head_size = weights.shape[2]
    normed = normed.reshape(-1, head_count, head_size)
    mapped = jnp.einsum("thd,khde->kthe", normed, weights, preferred_element_type=jnp.float32)
    queries = jax.nn.relu(mapped[0]).astype(jnp.bfloat16)
    key_rows = jax.nn.relu(mapped[1]).astype(jnp.bfloat16)
    value_rows = mapped[2].astype(jnp.bfloat16)
    gating = jax.nn.sigmoid(mapped[3])
    return (queries, key_rows, value_rows, gating)


def local_state(key_rows, value_rows):
    return jnp.einsum("thd,the->hde", key_rows, value_rows, preferred_element_type=jnp.float32)


def attend(queries, state):
    return jnp.einsum(
        "thd,hde->the", queries.astype(jnp.float32), state, precision=lax.Precision.HIGHEST
    )


def finish(frame_block, gating, attended):
    inv_rms = lax.rsqrt(jnp.mean(attended * attended, axis=-1, keepdims=True) + 1e-05)
    branch = (gating * attended * inv_rms).reshape(frame_block.shape)
    return (frame_block.astype(jnp.float32) + branch).astype(jnp.bfloat16)


def add_states(earlier, later):
    return earlier + later


def body(latents, spatial_weights, causal_weights):
    queries, key_rows, value_rows, gating = project(normalize(latents), spatial_weights)
    frame_state = lax.psum(local_state(key_rows, value_rows), "row")
    mixed_video = finish(latents, gating, attend(queries, frame_state))
    normed_c = normalize(mixed_video)
    mixed_heads, normed_heads = (
        lax.all_to_all(mixed_video, "row", split_axis=3, concat_axis=1, tiled=True),
        lax.all_to_all(normed_c, "row", split_axis=3, concat_axis=1, tiled=True),
    )
    head_part = causal_weights.shape[1] // lax.axis_size("row")
    head_start = lax.axis_index("row") * head_part
    local_weights = lax.dynamic_slice_in_dim(causal_weights, head_start, head_part, 1)
    queries, key_rows, value_rows, gating = project(normed_heads, local_weights)
    own_state = local_state(key_rows, value_rows)
    flat_state = own_state.reshape(-1, 128)
    earlier_flat = prefix(flat_state, "frame", add_states, jnp.zeros_like(flat_state))
    earlier = earlier_flat.reshape(own_state.shape)
    attended = attend(queries, earlier + own_state)
    return finish(mixed_heads, gating, attended)


def solution(mesh):
    in_specs = (P(("group", "frame"), "row", None, None), P(), P())
    out_specs = P(("group", "frame"), None, None, "row")
    return jax.shard_map(body, mesh=mesh, in_specs=in_specs, out_specs=out_specs, check_vma=False)
```

profile of v0, /device:TPU:27, one launch (start us, length us, event | category | flops | bytes accessed | tf_op | source)
XLA Modules:
  0.0 119.3 jit_solution(12640229504760504047)
XLA Ops:
  6.5 0.0 copy-start
  6.5 0.0 all-reduce.2.cloned.1.call-start
  6.5 1.6 %reshape.152 = f32[128,10,112]{2,1,0:T(8,128)S(1)} reshape(bf16[1,4,32,1120]{3,2,1,0:T(8,128)(2,1)} %param.5) | data formatting | bytes 860160 | tf_op jit(solution)/shard_map/convert_element_type | solution.py:20
  8.2 1.1 multiply_reduce_fusion
  9.3 0.1 rsqrt.36
  9.4 0.2 fusion.20
  9.6 0.0 copy-done
  9.6 0.5 convolution_bitcast_fusion.1
  10.1 1.1 fusion.24
  11.3 0.0 all-reduce.2.cloned.1.call-update
  11.3 20.5 %all-reduce.2.cloned.1.call-done = f32[10,112,112]{2,1,0:T(8,128)} async-done(((f32[10,112,112]{2,1,0:T(8,128)}), f32[10,112,112]{2,1,0:T(8,128)}) %all-reduce.2.cloned.1.call-update) | async-done | bytes 501776 | tf_op jit(solution)/shard_map/psum | solution.py:59
  31.8 1.7 %multiply_reduce_fusion.2 = (f32[128,10]{0,1:T(8,128)S(1)}, f32[128,10,112]{0,2,1:T(8,128)S(1)}) fusion(f32[10,112,112]{2,1,0:T(8,128)} %all-reduce.2.cloned.1.call-done, f32[4,128,10,112]{1,3,0,2:T(8,128)S(1)} %convolution_bitcast_fusion.1), kind=kOutput, calls=%fused_computation.40 | convolution fusion | flops 193391360 | bytes 1367040 | tf_op jit(solution)/shard_map/thd,hde->the/dot_general | solution.py:42
  33.5 1.0 fusion.18
  34.5 0.0 copy-start.2
  34.5 1.6 %copy.24 = f32[128,10,112]{2,1,0:T(8,128)S(1)} copy(f32[128,10,112]{0,2,1:T(8,128)} %fusion.18) | data formatting | bytes 1146880 | tf_op jit(solution)/shard_map/mul | solution.py:49
  36.1 0.3 reshape.147
  36.4 0.0 copy-done.2
  36.4 0.2 fusion.1
  36.6 1.4 %copy.25 = bf16[1,4,32,1120]{2,1,0,3:T(4,128)(2,1)S(1)} copy(bf16[1,4,32,1120]{3,2,1,0:T(8,128)(2,1)S(1)} %get-tuple-element.38) | data formatting | bytes 573440 | tf_op jit(solution)/shard_map/convert_element_type | solution.py:50
  38.0 0.8 fusion.2
  38.8 2.2 %copy.28 = bf16[1,4,32,1120]{2,1,0,3:T(4,128)(2,1)S(1)} copy(bf16[1,4,32,1120]{3,2,1,0:T(8,128)(2,1)} %fusion.2) | data formatting | bytes 573440 | tf_op jit(solution)/shard_map/convert_element_type | solution.py:22
  41.0 1.8 %reshape.159 = bf16[2,2,35840]{2,1,0:T(2,128)(2,1)} reshape(bf16[1120,1,4,32]{3,2,1,0:T(4,128)(2,1)S(1)} %bitcast.72) | data formatting | bytes 573440
  42.8 5.7 %all_to_all.24 = bf16[2,2,35840]{2,1,0:T(2,128)(2,1)} all-to-all(bf16[2,2,35840]{2,1,0:T(2,128)(2,1)} %reshape.159), channel_id=1, replica_groups=mesh['group'=2,'frame'=8,'row'=2] {'row'}, dimensions={0} | all-to-all | bytes 573440 | tf_op jit(solution)/shard_map/all_to_all | solution.py:64
  48.5 1.7 %reshape.160 = bf16[1120,1,4,32]{3,2,1,0:T(4,128)(2,1)S(1)} reshape(bf16[2,2,35840]{2,1,0:T(2,128)(2,1)} %all_to_all.24) | data formatting | bytes 573440
  50.2 1.4 %copy.29 = bf16[1,4,32,2,560]{4,2,1,3,0:T(8,128)(2,1)} copy(bf16[1,4,32,2,560]{2,1,4,3,0:T(4,128)(2,1)S(1)} %bitcast.73) | data formatting | bytes 573440 | tf_op jit(solution)/shard_map/all_to_all | solution.py:64
  51.5 1.4 %reshape.148 = bf16[256,5,112]{2,1,0:T(8,128)(2,1)S(1)} reshape(bf16[1,2,4,32,560]{4,3,2,1,0:T(8,128)(2,1)} %bitcast.76) | data formatting | bytes 573440 | tf_op jit(solution)/shard_map/reshape | solution.py:28
  52.9 1.6 %convolution_bitcast_fusion = f32[4,256,5,112]{1,3,0,2:T(8,128)S(1)} fusion(bf16[256,5,112,1]{2,1,0,3:T(8,128)(2,1)S(1)} %bitcast.75, bf16[4,10,112,112]{3,2,1,0:T(8,128)(2,1)} %param.7, s32[]{:T(128)S(6)} %select_n.7), kind=kOutput, calls=%fused_computation.1 | convolution fusion | flops 128450560 | bytes 3153924 | tf_op jit(solution)/shard_map/thd,khde->kthe/dot_general | solution.py:29
  54.5 0.0 copy-start.1
  54.5 1.4 %copy-done.1 = f32[4,256,5,112]{1,3,0,2:T(8,128)} copy-done((f32[4,256,5,112]{1,3,0,2:T(8,128)}, f32[4,256,5,112]{1,3,0,2:T(8,128)S(1)}, u32[]{:S(2)}) %copy-start.1) | copy-done | bytes 2293784
  55.9 0.2 fusion.46
  56.1 0.3 convert_element_type.131
  56.4 28.5 %all_gather.4 = bf16[8,490,128]{2,1,0:T(8,128)(2,1)} all-gather(bf16[1,490,128]{2,1,0:T(8,128)(2,1)S(1)} %convert_element_type.131), channel_id=1, replica_groups=mesh['group'=2,'frame'=8,'row'=2] {'frame'}, dimensions={0}, use_global_device_ids=true | all-gather | bytes 1128960 | tf_op jit(solution)/shard_map/all_gather | solution.py:9
  84.9 6.8 %while.10 = (s32[]{:T(128)}, f32[490,128]{1,0:T(8,128)S(1)}, s32[]{:T(128)}, bf16[8,490,128]{2,1,0:T(8,128)(2,1)}, s32[]{:T(128)}, /*index=5*/s32[]{:T(128)}, s32[]{:T(128)}) while((s32[]{:T(128)}, f32[490,128]{1,0:T(8,128)S(1)}, s32[]{:T(128)}, bf16[8,490,128]{2,1,0:T(8,128)(2,1)}, s32[]{:T(128)}, /*index=5*/s32[]{:T(128)}, s32[]{:T(128)}) %tuple.22), condition=%wide.region_5.6_spmd, body=%wide.region_4.5_spmd.sunk | while | flops 125445 | bytes 627315 | solution.py:15
  85.0 0.9 convert_add_fusion.2
  85.9 0.9 convert_add_fusion.2
  86.9 0.9 convert_add_fusion.2
  87.9 0.9 convert_add_fusion.2
  88.8 0.9 convert_add_fusion.2
  89.8 0.9 convert_add_fusion.2
  90.8 0.9 convert_add_fusion.2
  91.7 0.2 reshape.149
  91.9 1.5 %multiply_reduce_fusion.1 = (f32[256,5]{0,1:T(8,128)S(1)}, f32[256,5,112]{0,2,1:T(8,128)S(1)}) fusion(f32[4,256,5,112]{1,3,0,2:T(8,128)} %copy-done.1, f32[5,112,112]{2,1,0:T(8,128)S(1)} %reshape.149, f32[5,112,112]{2,1,0:T(8,128)S(1)} %get-tuple-element.42), kind=kOutput, calls=%fused_computation.39 | convolution fusion | flops 193454080 | bytes 1367040 | tf_op jit(solution)/shard_map/thd,hde->the/dot_general | solution.py:42
  93.5 2.0 %fusion.10 = f32[256,5,112]{0,2,1:T(8,128)} fusion(f32[256,5,112]{0,2,1:T(8,128)S(1)} %get-tuple-element.44, f32[4,256,5,112]{1,3,0,2:T(8,128)} %copy-done.1, f32[256,5]{0,1:T(8,128)S(1)} %add_rsqrt_fusion), kind=kLoop, calls=%fused_computation.25 | loop fusion | flops 716800 | bytes 1725440 | tf_op jit(solution)/shard_map/mul | solution.py:49
  95.5 1.5 %copy.32 = f32[256,5,112]{2,1,0:T(8,128)S(1)} copy(f32[256,5,112]{0,2,1:T(8,128)} %fusion.10) | data formatting | bytes 1146880 | tf_op jit(solution)/shard_map/mul | solution.py:49
  97.0 1.1 reshape.150
  98.0 1.1 reshape.157
  99.2 10.2 %all_to_all.25 = bf16[2,2,35840]{2,1,0:T(2,128)(2,1)S(1)} all-to-all(bf16[2,2,35840]{2,1,0:T(2,128)(2,1)S(1)} %reshape.157), channel_id=1, replica_groups=mesh['group'=2,'frame'=8,'row'=2] {'row'}, dimensions={0} | all-to-all | bytes 573440 | tf_op jit(solution)/shard_map/all_to_all | solution.py:63
  109.3 0.6 reshape.158
  109.9 0.7 copy.26
  110.6 1.9 %add_convert_fusion = bf16[1,8,32,560]{3,2,1,0:T(8,128)(2,1)} fusion(f32[1,8,32,560]{3,2,1,0:T(8,128)S(1)} %bitcast.74, f32[1,8,32,560]{3,2,1,0:T(8,128)} %reshape.150), kind=kLoop, calls=%fused_computation.9 | loop fusion | flops 286720 | bytes 1433600 | tf_op jit(solution)/shard_map/convert_element_type | solution.py:50
  (5 shorter events, 0.0 us)
Async XLA Ops:
  6.5 3.1 %copy-start = (bf16[4,10,112,112]{3,2,1,0:T(8,128)(2,1)S(1)}, bf16[4,10,112,112]{3,2,1,0:T(8,128)(2,1)}, u32[]{:S(2)}) copy-start(bf16[4,10,112,112]{3,2,1,0:T(8,128)(2,1)} %param.6) | copy-start | bytes 3010564
  6.5 25.2 %all-reduce.2.cloned.1.call-start = ((), (), s32[]{:S(2)}) async-start(), calls=%async_computation.2 | async-start | bytes 1146880 | tf_op jit(solution)/shard_map/psum | solution.py:59
  34.5 1.9 %copy-start.2 = (bf16[1,4,32,1120]{3,2,1,0:T(8,128)(2,1)S(1)}, bf16[1,4,32,1120]{3,2,1,0:T(8,128)(2,1)}, u32[]{:S(2)}) copy-start(bf16[1,4,32,1120]{3,2,1,0:T(8,128)(2,1)} %param.5) | copy-start | bytes 860164
  54.5 1.4 %copy-start.1 = (f32[4,256,5,112]{1,3,0,2:T(8,128)}, f32[4,256,5,112]{1,3,0,2:T(8,128)S(1)}, u32[]{:S(2)}) copy-start(f32[4,256,5,112]{1,3,0,2:T(8,128)S(1)} %convolution_bitcast_fusion) | copy-start | bytes 6881284
Sparse Core Ops, SparseCore 0:
  11.4 20.3 all-reduce.1
where the time goes:
time: 120 us; the launch traced here: 119 us
  blocking collectives  44.3 us (37%)
  waiting for transfers between devices  20.5 us (17%)
  local copies, waits for them, and re-layouts  20.1 us (17%)
  other arithmetic  13.8 us (12%)
  between operations  13.6 us (11%)
  matrix products  6.67 us (6%)
    all_gather x1, blocking collectives, prefix(): gathered = lax.all_gather(x.astype(jnp.bfloat16), axis)  28.5 us
    psum x1, waiting for transfers between devices, body(): frame_state = lax.psum(local_state(key_rows, value_rows), 'row')  20.5 us
    all_to_all x1, blocking collectives, body(): lax.all_to_all(mixed_video, 'row', split_axis=3, concat_axis=1, tiled=True)  10.2 us
    add x7, other arithmetic, add_states(): return earlier + later  6.6 us
    unnamed x10, local copies, waits for them, and re-layouts  6.55 us
    all_to_all x1, blocking collectives, body(): lax.all_to_all(normed_c, 'row', split_axis=3, concat_axis=1, tiled=True)  5.67 us
    dot_general x2, matrix products, attend(): jnp.einsum('thd,hde->the', queries.astype(jnp.float32), state, precision=...  3.21 us
    mul x2, local copies, waits for them, and re-layouts, finish(): branch = (gating * attended * inv_rms).reshape(frame_block.shape)  3.07 us
  transfers between devices with their start and end apart: 1, of which 1 were waited for; matrix products, arithmetic and copies ran while one was open for 0% of the time, Pallas kernels for 0%

commit v1 on v0

--- a/solution.py
+++ b/solution.py
@@ -56,7 +56,7 @@
 
 def body(latents, spatial_weights, causal_weights):
     queries, key_rows, value_rows, gating = project(normalize(latents), spatial_weights)
-    frame_state = lax.psum(local_state(key_rows, value_rows), "row")
+    frame_state = jnp.sum(lax.all_gather(local_state(key_rows, value_rows), "row"), axis=0)
     mixed_video = finish(latents, gating, attend(queries, frame_state))
     normed_c = normalize(mixed_video)
     mixed_heads, normed_heads = (

time: 120 us -> 75.4 us (0.63)
  the two profiles are of different devices: /device:TPU:27 before, /device:TPU:0 now
where the time goes in v1:
time: 75.4 us; the launch traced here: 74.8 us
  blocking collectives  37.6 us (50%)
  local copies, waits for them, and re-layouts  16.3 us (22%)
  other arithmetic  7.94 us (11%)
  starting transfers between devices  6.9 us (9%)
  matrix products  5.85 us (8%)
    all_gather x1, blocking collectives, prefix(): gathered = lax.all_gather(x.astype(jnp.bfloat16), axis)  34.7 us
    unnamed x10, local copies, waits for them, and re-layouts  6.14 us
    all_to_all x1, starting transfers between devices, body(): lax.all_to_all(mixed_video, 'row', split_axis=3, concat_axis=1, tiled=True)  3.45 us
    all_to_all x1, starting transfers between devices, body(): lax.all_to_all(normed_c, 'row', split_axis=3, concat_axis=1, tiled=True)  3.45 us
    dot_general x2, matrix products, attend(): jnp.einsum('thd,hde->the', queries.astype(jnp.float32), state, precision=...  3.21 us
    all_gather x1, blocking collectives, body(): lax.all_gather(local_state(key_rows, value_rows), 'row')  2.87 us
    reduce_sum x1, other arithmetic, body(): jnp.sum(lax.all_gather(local_state(key_rows, value_rows), 'row'), axis=0)  2.23 us
    mul x2, other arithmetic, finish(): branch = (gating * attended * inv_rms).reshape(frame_block.shape)  2.19 us
  transfers between devices with their start and end apart: 2, of which 0 were waited for; matrix products, arithmetic and copies ran while one was open for 15% of the time, Pallas kernels for 0%

profile of v1, /device:TPU:0, one launch (start us, length us, event | category | flops | bytes accessed | tf_op | source)
XLA Modules:
  0.0 74.8 jit_solution(14493470499125631938)
XLA Ops:
  0.0 0.0 copy-start
  0.0 1.6 %reshape.152 = f32[128,10,112]{2,1,0:T(8,128)S(1)} reshape(bf16[1,4,32,1120]{3,2,1,0:T(8,128)(2,1)} %param.5) | data formatting | bytes 860160 | tf_op jit(solution)/shard_map/convert_element_type | solution.py:20
  1.6 1.1 %multiply_reduce_fusion = f32[4,32]{1,0:T(4,128)S(1)} fusion(bf16[1,4,32,1120]{3,2,1,0:T(8,128)(2,1)} %param.5), kind=kLoop, calls=%fused_computation.13 | loop fusion | flops 429952 | bytes 287232 | tf_op jit(solution)/shard_map/reduce_sum | solution.py:21
  2.7 0.1 rsqrt.36
  2.8 0.2 fusion.20
  3.1 0.0 copy-done
  3.1 0.5 convolution_bitcast_fusion.1
  3.6 0.3 fusion.24
  3.9 2.9 %all-gather = f32[20,112,112]{2,1,0:T(8,128)} all-gather(f32[10,112,112]{2,1,0:T(8,128)S(1)} %fusion.24), channel_id=2, replica_groups=mesh['group'=2,'frame'=8,'row'=2] {'row'}, dimensions={0}, use_global_device_ids=true | all-gather | bytes 1505280 | tf_op jit(solution)/shard_map/all_gather | solution.py:59
  6.8 2.2 %reduce_sum.46 = f32[10,112,112]{2,1,0:T(8,128)} reduce(f32[2,10,112,112]{3,2,1,0:T(8,128)} %bitcast.72, f32[]{:T(128)} %constant.18.clone.1), dimensions={0}, to_apply=%region_1.2 | reduce | flops 125440 | bytes 1505284 | tf_op jit(solution)/shard_map/reduce_sum | solution.py:59
  9.0 1.7 %multiply_reduce_fusion.2 = (f32[128,10]{0,1:T(8,128)S(1)}, f32[128,10,112]{0,2,1:T(8,128)S(1)}) fusion(f32[10,112,112]{2,1,0:T(8,128)} %reduce_sum.46, f32[4,128,10,112]{1,3,0,2:T(8,128)S(1)} %convolution_bitcast_fusion.1), kind=kOutput, calls=%fused_computation.40 | convolution fusion | flops 193391360 | bytes 1367040 | tf_op jit(solution)/shard_map/thd,hde->the/dot_general | solution.py:42
  10.7 1.0 %fusion.18 = f32[128,10,112]{0,2,1:T(8,128)} fusion(f32[128,10,112]{0,2,1:T(8,128)S(1)} %get-tuple-element.40, f32[4,128,10,112]{1,3,0,2:T(8,128)S(1)} %convolution_bitcast_fusion.1, f32[128,10]{0,1:T(8,128)S(1)} %add_rsqrt_fusion.1), kind=kLoop, calls=%fused_computation.37 | loop fusion | flops 716800 | bytes 1725440 | tf_op jit(solution)/shard_map/mul | solution.py:49
  11.7 0.0 copy-start.2
  11.7 1.6 %copy.24 = f32[128,10,112]{2,1,0:T(8,128)S(1)} copy(f32[128,10,112]{0,2,1:T(8,128)} %fusion.18) | data formatting | bytes 1146880 | tf_op jit(solution)/shard_map/mul | solution.py:49
  13.3 0.3 reshape.147
  13.6 0.0 copy-done.2
  13.6 0.2 fusion.1
  13.8 0.1 fusion.2
  13.9 1.4 %copy.28 = bf16[1,4,32,1120]{2,1,0,3:T(4,128)(2,1)S(1)} copy(bf16[1,4,32,1120]{3,2,1,0:T(8,128)(2,1)S(1)} %fusion.2) | data formatting | bytes 573440 | tf_op jit(solution)/shard_map/convert_element_type | solution.py:22
  15.3 1.8 %reshape.160 = bf16[2,2,35840]{2,1,0:T(2,128)(2,1)} reshape(bf16[1120,1,4,32]{3,2,1,0:T(4,128)(2,1)S(1)} %bitcast.73) | data formatting | bytes 573440
  17.1 3.4 %all-to-all-start.1 = ((bf16[2,2,35840]{2,1,0:T(2,128)(2,1)}), bf16[2,2,35840]{2,1,0:T(2,128)(2,1)S(1)}, u32[]{:S(2)}, u32[]{:S(2)}) async-start(bf16[2,2,35840]{2,1,0:T(2,128)(2,1)} %reshape.160), calls=%async_computation.1 | async-start | bytes 573440 | tf_op jit(solution)/shard_map/all_to_all | solution.py:64
  20.6 1.4 %copy.25 = bf16[1,4,32,1120]{2,1,0,3:T(4,128)(2,1)S(1)} copy(bf16[1,4,32,1120]{3,2,1,0:T(8,128)(2,1)S(1)} %get-tuple-element.38) | data formatting | bytes 573440 | tf_op jit(solution)/shard_map/convert_element_type | solution.py:50
  22.0 1.8 %reshape.158 = bf16[2,2,35840]{2,1,0:T(2,128)(2,1)} reshape(bf16[1120,1,4,32]{3,2,1,0:T(4,128)(2,1)S(1)} %bitcast.74) | data formatting | bytes 573440
  23.8 0.0 all-to-all-done.1
  23.8 3.4 %all-to-all-start = ((bf16[2,2,35840]{2,1,0:T(2,128)(2,1)}), bf16[2,2,35840]{2,1,0:T(2,128)(2,1)S(1)}, u32[]{:S(2)}, u32[]{:S(2)}) async-start(bf16[2,2,35840]{2,1,0:T(2,128)(2,1)} %reshape.158), calls=%async_computation | async-start | bytes 573440 | tf_op jit(solution)/shard_map/all_to_all | solution.py:63
  27.3 0.6 reshape.161
  27.9 0.7 copy.29
  28.6 0.4 reshape.148
  29.0 1.6 %convolution_bitcast_fusion = f32[4,256,5,112]{1,3,0,2:T(8,128)S(1)} fusion(bf16[256,5,112,1]{2,1,0,3:T(8,128)(2,1)S(1)} %bitcast.77, bf16[4,10,112,112]{3,2,1,0:T(8,128)(2,1)} %param.7, s32[]{:T(128)S(6)} %select_n.7), kind=kOutput, calls=%fused_computation.1 | convolution fusion | flops 128450560 | bytes 3153924 | tf_op jit(solution)/shard_map/thd,khde->kthe/dot_general | solution.py:29
  30.6 0.0 copy-start.1
  30.6 1.4 %copy-done.1 = f32[4,256,5,112]{1,3,0,2:T(8,128)} copy-done((f32[4,256,5,112]{1,3,0,2:T(8,128)}, f32[4,256,5,112]{1,3,0,2:T(8,128)S(1)}, u32[]{:S(2)}) %copy-start.1) | copy-done | bytes 2293784
  32.0 0.2 fusion.46
  32.2 0.3 convert_element_type.131
  32.5 34.7 %all_gather.12 = bf16[8,490,128]{2,1,0:T(8,128)(2,1)S(1)} all-gather(bf16[1,490,128]{2,1,0:T(8,128)(2,1)S(1)} %convert_element_type.131), channel_id=1, replica_groups=mesh['group'=2,'frame'=8,'row'=2] {'frame'}, dimensions={0}, use_global_device_ids=true | all-gather | bytes 1128960 | tf_op jit(solution)/shard_map/all_gather | solution.py:9
  67.2 0.2 reshape.149
  67.4 1.5 %multiply_reduce_fusion.1 = (f32[256,5]{0,1:T(8,128)S(1)}, f32[256,5,112]{0,2,1:T(8,128)S(1)}) fusion(f32[4,256,5,112]{1,3,0,2:T(8,128)} %copy-done.1, f32[5,112,112]{2,1,0:T(8,128)S(1)} %reshape.149, f32[5,112,112]{2,1,0:T(8,128)S(1)} %get-tuple-element.42), kind=kOutput, calls=%fused_computation.39 | convolution fusion | flops 193454080 | bytes 1367040 | tf_op jit(solution)/shard_map/thd,hde->the/dot_general | solution.py:42
  68.9 1.2 %fusion.10 = f32[256,5,112]{0,2,1:T(8,128)S(1)} fusion(f32[256,5,112]{0,2,1:T(8,128)S(1)} %get-tuple-element.44, f32[4,256,5,112]{1,3,0,2:T(8,128)} %copy-done.1, f32[256,5]{0,1:T(8,128)S(1)} %add_rsqrt_fusion), kind=kLoop, calls=%fused_computation.25 | loop fusion | flops 716800 | bytes 1725440 | tf_op jit(solution)/shard_map/mul | solution.py:49
  70.2 0.4 copy.32
  70.6 1.1 %reshape.150 = f32[1,8,32,560]{3,2,1,0:T(8,128)} reshape(f32[256,5,112]{2,1,0:T(8,128)S(1)} %copy.32) | data formatting | bytes 1146880 | tf_op jit(solution)/shard_map/reshape | solution.py:49
  71.6 0.0 all-to-all-done
  71.6 0.6 reshape.159
  72.2 0.7 copy.26
  72.9 1.9 %add_convert_fusion = bf16[1,8,32,560]{3,2,1,0:T(8,128)(2,1)} fusion(f32[1,8,32,560]{3,2,1,0:T(8,128)S(1)} %bitcast.76, f32[1,8,32,560]{3,2,1,0:T(8,128)} %reshape.150), kind=kLoop, calls=%fused_computation.9 | loop fusion | flops 286720 | bytes 1433600 | tf_op jit(solution)/shard_map/convert_element_type | solution.py:50
  (6 shorter events, 0.1 us)
Async XLA Ops:
  0.0 3.1 %copy-start = (bf16[4,10,112,112]{3,2,1,0:T(8,128)(2,1)S(1)}, bf16[4,10,112,112]{3,2,1,0:T(8,128)(2,1)}, u32[]{:S(2)}) copy-start(bf16[4,10,112,112]{3,2,1,0:T(8,128)(2,1)} %param.6) | copy-start | bytes 3010564
  11.7 1.9 %copy-start.2 = (bf16[1,4,32,1120]{3,2,1,0:T(8,128)(2,1)S(1)}, bf16[1,4,32,1120]{3,2,1,0:T(8,128)(2,1)}, u32[]{:S(2)}) copy-start(bf16[1,4,32,1120]{3,2,1,0:T(8,128)(2,1)} %param.5) | copy-start | bytes 860164
  17.1 6.7 %all-to-all-start.1 = ((bf16[2,2,35840]{2,1,0:T(2,128)(2,1)}), bf16[2,2,35840]{2,1,0:T(2,128)(2,1)S(1)}, u32[]{:S(2)}, u32[]{:S(2)}) async-start(bf16[2,2,35840]{2,1,0:T(2,128)(2,1)} %reshape.160), calls=%async_computation.1 | async-start | bytes 573440 | tf_op jit(solution)/shard_map/all_to_all | solution.py:64
  23.8 47.8 %all-to-all-start = ((bf16[2,2,35840]{2,1,0:T(2,128)(2,1)}), bf16[2,2,35840]{2,1,0:T(2,128)(2,1)S(1)}, u32[]{:S(2)}, u32[]{:S(2)}) async-start(bf16[2,2,35840]{2,1,0:T(2,128)(2,1)} %reshape.158), calls=%async_computation | async-start | bytes 573440 | tf_op jit(solution)/shard_map/all_to_all | solution.py:63
  30.6 1.4 %copy-start.1 = (f32[4,256,5,112]{1,3,0,2:T(8,128)}, f32[4,256,5,112]{1,3,0,2:T(8,128)S(1)}, u32[]{:S(2)}) copy-start(f32[4,256,5,112]{1,3,0,2:T(8,128)S(1)} %convolution_bitcast_fusion) | copy-start | bytes 6881284
